TPU v7x, 256 devices: a whole 4x4x8 slice. The times are simulated.
256 devices in a mesh: row: 16 (over x, y), col: 16 (over z, core).
Axes of the slice: x: 4, y: 4, z: 8, core: 2. Of those that a mesh axis runs over, the one named last changes fastest.
Arguments:
- root_block: bfloat16 [16, 256, 4096], P('row', None, 'col'), may hold values from -1 to 3, as said below
- l_one: bfloat16 [16, 256, 4096], P('row', None, 'col'), may hold values from -0.09375 to 0.09375
- dinv_one: bfloat16 [16, 128, 4096], P('row', None, 'col'), may hold values from -1 to 3, as said below
- l_two: bfloat16 [16, 384, 4096], P('row', None, 'col'), may hold values from -0.078125 to 0.078125
- dinv_two: bfloat16 [16, 64, 4096], P('row', None, 'col'), may hold values from -1 to 3, as said below
- l_three: bfloat16 [16, 448, 4096], P('row', None, 'col'), may hold values from -0.0625 to 0.0625
- dinv_three: bfloat16 [16, 32, 4096], P('row', None, 'col'), may hold values from -1 to 3, as said below
Outputs:
- sigma_one: float32 [16, 384, 4096], P('row', None, 'col')
- sigma_two: float32 [16, 448, 4096], P('row', None, 'col')
- sigma_three: float32 [16, 480, 4096], P('row', None, 'col')
Inputs may be any that keep to these rules, and one draw needn't show every extreme that they name: Each node's diagonal block of root_block (in natural row order, in the node's columns) is exactly symmetric. `dinv_one`: each node's 2048 x 2048 block in natural row order is exactly symmetric. `dinv_two`: each node's 1024 x 1024 block in natural row order is exactly symmetric. `dinv_three`: each node's 512 x 512 block in natural row order is exactly symmetric.
All inputs are finite; a program needn't handle non-finite values.
Results may differ from a plain program's by a relative error of at most 0.0003.
Values may be sent and summed in bfloat16 or wider, within the bound.
A program may use at most 64 MiB of HBM per device.

v0:
```python
import jax
import jax.numpy as jnp
from jax import lax
from jax.sharding import PartitionSpec as P

S0 = 4096
S1 = 2048
S2 = 1024
S3 = 512


exact_mode = lax.Precision.HIGHEST


def swapped(value, axis, apart):
    mask = 2**apart
    pairs = [(source, source ^ mask) for source in range(lax.axis_size(axis))]
    return lax.ppermute(value, axis, pairs)


def product(left_side, right_side):
    return jnp.dot(left_side, right_side, precision=exact_mode, preferred_element_type=jnp.float32)


def transposed_product(left_side, right_side):
    return lax.dot_general(
        left_side,
        right_side,
        (((0,), (0,)), ((), ())),
        precision=exact_mode,
        preferred_element_type=jnp.float32,
    )


def doubling_order(own_tile, partner, position):
    column = lax.axis_index("col")
    higher = column // 2**position % 2 == 1
    return jnp.where(
        higher, jnp.concatenate([partner, own_tile], 1), jnp.concatenate([own_tile, partner], 1)
    )


def collect_panel(panel_tile, group_size):
    for position in range(group_size.bit_length() - 1):
        partner = swapped(panel_tile, "col", position)
        panel_tile = doubling_order(panel_tile, partner, position)
    return panel_tile


def per_device(root_block, l_one, dinv_one, l_two, dinv_two, l_three, dinv_three):
    run_count = lax.axis_size("row")
    tile_width = root_block.shape[2]
    block_widths = [S0, S1, S2, S3]
    run_rows = [block_width // run_count for block_width in block_widths]
    row_offsets = [
        0,
        run_rows[0],
        run_rows[0] + run_rows[1],
        run_rows[0] + run_rows[1] + run_rows[2],
    ]
    factors = [l_one[0], l_two[0], l_three[0]]
    inverses = [dinv_one[0], dinv_two[0], dinv_three[0]]
    root_rows = lax.all_gather(root_block[0], "col", axis=1, tiled=True)
    panels = [root_rows]
    crossed = [root_rows]
    outputs = []
    for tree_level in range(1, 4):
        factor_tile = factors[tree_level - 1]
        head_rows = row_offsets[tree_level]
        gathered = lax.all_gather(factor_tile, "row", axis=0, tiled=True)
        stacked = gathered.reshape(run_count, head_rows, tile_width)
        running = jnp.zeros((head_rows, tile_width), jnp.float32)
        for block_index in range(tree_level):
            natural_part = stacked[
                :, row_offsets[block_index] : row_offsets[block_index + 1], :
            ].reshape(block_widths[block_index], tile_width)
            if block_index == 0:
                term_rows = jnp.dot(panels[0], natural_part, preferred_element_type=jnp.float32)
            else:
                term_rows = product(panels[block_index], natural_part.astype(jnp.float32))
            running = running + jnp.pad(term_rows, ((0, head_rows - term_rows.shape[0]), (0, 0)))
        factor_float = factor_tile.astype(jnp.float32)
        if tree_level > 1:
            pieces = []
            for block_index in range(1, tree_level):
                partial_sum = transposed_product(
                    panels[block_index][: row_offsets[block_index]],
                    factor_float[: row_offsets[block_index]],
                )
                pieces.append(partial_sum.reshape(run_count, run_rows[block_index], tile_width))
            joined = jnp.concatenate(pieces, 1).reshape(
                run_count * (head_rows - row_offsets[1]), tile_width
            )
            reduced = lax.psum_scatter(joined, "row", scatter_dimension=0, tiled=True)
            running = running + jnp.pad(reduced, ((row_offsets[1], 0), (0, 0)))
        panel_rows = -running
        inverse_tile = inverses[tree_level - 1].astype(jnp.float32)
        group_size = block_widths[tree_level] // tile_width
        spread = collect_panel(panel_rows, group_size)
        diag_terms = transposed_product(spread, factor_float)
        diag_rows = inverse_tile - lax.psum_scatter(
            diag_terms, "row", scatter_dimension=0, tiled=True
        )
        sigma_tile = jnp.concatenate([panel_rows, diag_rows], 0)
        outputs.append(sigma_tile[None])
        if tree_level < 3:
            whole_panel = jnp.concatenate([spread, collect_panel(diag_rows, group_size)], 0)
            panels.append(whole_panel)
            crossed.append(whole_panel)
    return (outputs[0], outputs[1], outputs[2])


def solution(mesh):
    placed = (
        P("row", None, "col"),
        P("row", None, "col"),
        P("row", None, "col"),
        P("row", None, "col"),
        P("row", None, "col"),
        P("row", None, "col"),
        P("row", None, "col"),
    )
    return jax.shard_map(
        per_device,
        mesh=mesh,
        in_specs=placed,
        out_specs=(P("row", None, "col"), P("row", None, "col"), P("row", None, "col")),
        check_vma=False,
    )
```

profile of v0, /device:TPU:24, one launch (start us, length us, event | category | flops | bytes accessed | tf_op | source)
XLA Modules:
  0.0 704.9 jit_solution(9191428733446846489)
XLA Ops:
  8.7 44.7 %all-gather.9.cloned.1.call-done = bf16[1,256,4096]{2,1,0:T(8,128)(2,1)} async-done(((bf16[1,256,256]{2,1,0:T(8,128)(2,1)}), bf16[1,256,4096]{2,1,0:T(8,128)(2,1)}) %all-gather.9.cloned.1.call-update) | async-done | bytes 2097168 | tf_op jit(solution)/shard_map/all_gather | solution.py:63
  53.4 51.2 %all-gather.11.cloned.1.call-done = bf16[1,4096,256]{2,1,0:T(8,128)(2,1)} async-done(((bf16[1,256,256]{2,1,0:T(8,128)(2,1)}), bf16[1,4096,256]{2,1,0:T(8,128)(2,1)}) %all-gather.11.cloned.1.call-update) | async-done | bytes 2097168 | tf_op jit(solution)/shard_map/all_gather | solution.py:70
  104.6 3.1 fusion.25
  107.9 1.5 collective-permute-done
  109.4 1.6 collective-permute-start.1
  111.1 12.4 %collective-permute-done.1 = f32[256,512]{0,1:T(8,128)S(1)} collective-permute-done((f32[256,512]{0,1:T(8,128)S(1)}, f32[256,512]{0,1:T(8,128)S(1)}, u32[]{:S(2)}, u32[]{:S(2)}) %collective-permute-start.1) | collective-permute-done | bytes 524320 | tf_op jit(solution)/shard_map/ppermute | solution.py:18
  123.6 2.6 collective-permute-start.2
  126.2 45.3 %collective-permute-done.2 = f32[256,1024]{0,1:T(8,128)} collective-permute-done((f32[256,1024]{0,1:T(8,128)S(1)}, f32[256,1024]{0,1:T(8,128)}, u32[]{:S(2)}, u32[]{:S(2)}) %collective-permute-start.2) | collective-permute-done | bytes 1048608 | tf_op jit(solution)/shard_map/ppermute | solution.py:18
  171.5 1.9 maximum_select_fusion
  173.4 2.6 fusion.47
  177.0 2.4 fusion.45
  180.3 74.8 %reduce-scatter.6.cloned.1.call-done = f32[128,256]{0,1:T(8,128)} async-done(((f32[2048,256]{0,1:T(8,128)}), f32[128,256]{0,1:T(8,128)}) %reduce-scatter.6.cloned.1.call-update) | async-done | bytes 131088 | tf_op jit(solution)/shard_map/reduce_scatter | solution.py:101
  255.1 0.9 convert_subtract_fusion
  256.1 1.3 collective-permute-done.3
  257.5 1.6 collective-permute-start.4
  259.1 6.8 collective-permute-done.4
  266.0 2.6 collective-permute-start.5
  268.6 41.1 %all-gather.13.cloned.1.call-done = bf16[1,6144,256]{2,1,0:T(8,128)(2,1)} async-done(((bf16[1,384,256]{2,1,0:T(8,128)(2,1)}), bf16[1,6144,256]{2,1,0:T(8,128)(2,1)}) %all-gather.13.cloned.1.call-update) | async-done | bytes 3145744 | tf_op jit(solution)/shard_map/all_gather | solution.py:70
  309.7 1.7 slice.44
  311.4 2.4 slice.45
  314.7 2.3 maximum_select_fusion.3
  317.0 75.3 %reduce-scatter.8.cloned.1.call-done = f32[128,256]{1,0:T(8,128)} async-done(((f32[2048,256]{1,0:T(8,128)}), f32[128,256]{1,0:T(8,128)}) %reduce-scatter.8.cloned.1.call-update) | async-done | bytes 131088 | tf_op jit(solution)/shard_map/reduce_scatter | solution.py:94
  392.3 4.2 fusion.24
  396.6 1.7 collective-permute-done.6
  398.3 1.8 collective-permute-start.7
  400.2 18.0 %collective-permute-done.7 = f32[384,512]{1,0:T(8,128)S(1)} collective-permute-done((f32[384,512]{1,0:T(8,128)S(1)}, f32[384,512]{1,0:T(8,128)S(1)}, u32[]{:S(2)}, u32[]{:S(2)}) %collective-permute-start.7) | collective-permute-done | bytes 786464 | tf_op jit(solution)/shard_map/ppermute | solution.py:18
  418.5 1.2 copy-done
  419.7 2.4 fusion.40
  422.2 2.4 fusion.43
  424.6 3.0 copy.16
  427.6 2.5 fusion.38
  430.2 2.0 pad_maximum_fusion.1
  432.2 16.3 %all-gather.15.cloned.1.call-done = bf16[1,7168,256]{2,1,0:T(8,128)(2,1)} async-done(((bf16[1,448,256]{2,1,0:T(8,128)(2,1)}), bf16[1,7168,256]{2,1,0:T(8,128)(2,1)}) %all-gather.15.cloned.1.call-update) | async-done | bytes 3670032 | tf_op jit(solution)/shard_map/all_gather | solution.py:70
  448.6 3.1 slice.46
  451.7 77.7 %reduce-scatter.10.cloned.1.call-done = f32[64,256]{1,0:T(8,128)} async-done(((f32[1024,256]{1,0:T(8,128)}), f32[64,256]{1,0:T(8,128)}) %reduce-scatter.10.cloned.1.call-update) | async-done | bytes 65552 | tf_op jit(solution)/shard_map/reduce_scatter | solution.py:101
  529.4 0.8 convert_subtract_fusion.1
  530.2 3.6 fusion.4
  533.9 1.4 slice.47
  535.2 1.1 slice.48
  536.4 1.6 collective-permute-start.9
  538.0 3.4 fusion
  541.4 0.9 collective-permute-done.9
  542.4 71.3 %reduce-scatter.12.cloned.1.call-done = f32[192,256]{1,0:T(8,128)} async-done(((f32[3072,256]{1,0:T(8,128)}), f32[192,256]{1,0:T(8,128)}) %reduce-scatter.12.cloned.1.call-update) | async-done | bytes 196624 | tf_op jit(solution)/shard_map/reduce_scatter | solution.py:94
  613.6 2.6 fusion.19
  616.3 1.8 collective-permute-done.10
  618.1 1.8 fusion.30
  620.0 0.9 copy.17
  621.7 75.0 %reduce-scatter.14.cloned.1.call-done = f32[32,256]{1,0:T(8,128)} async-done(((f32[512,256]{1,0:T(8,128)}), f32[32,256]{1,0:T(8,128)}) %reduce-scatter.14.cloned.1.call-update) | async-done | bytes 32784 | tf_op jit(solution)/shard_map/reduce_scatter | solution.py:101
  (64 shorter events, 7.5 us)
Async XLA Ops:
  7.2 46.3 %all-gather.9.cloned.1.call-start = ((), (), s32[]{:S(2)}) async-start(), calls=%async_computation.10 | async-start | bytes 2228224 | tf_op jit(solution)/shard_map/all_gather | solution.py:63
  7.9 96.7 %all-gather.11.cloned.1.call-start = ((), (), s32[]{:S(2)}) async-start(), calls=%async_computation.11 | async-start | bytes 2228224 | tf_op jit(solution)/shard_map/all_gather | solution.py:70
  8.6 246.5 %reduce-scatter.6.cloned.1.call-start = ((), (), s32[]{:S(2)}) async-start(), calls=%async_computation.5 | async-start | bytes 2228224 | tf_op jit(solution)/shard_map/reduce_scatter | solution.py:101
  107.8 1.6 collective-permute-start
  109.4 14.1 %collective-permute-start.1 = (f32[256,512]{0,1:T(8,128)S(1)}, f32[256,512]{0,1:T(8,128)S(1)}, u32[]{:S(2)}, u32[]{:S(2)}) collective-permute-start(f32[256,512]{0,1:T(8,128)S(1)} %maximum_select_fusion.7), channel_id=1, source_target_pairs={{0,2},{1,3},{2,0},{3,1},{4,6},{5,7},{6,4},{7,5},{8,10},{9,11},{10,... | collective-permute-start | bytes 1572872 | tf_op jit(solution)/shard_map/ppermute | solution.py:18
  123.6 47.9 %collective-permute-start.2 = (f32[256,1024]{0,1:T(8,128)S(1)}, f32[256,1024]{0,1:T(8,128)}, u32[]{:S(2)}, u32[]{:S(2)}) collective-permute-start(f32[256,1024]{0,1:T(8,128)S(1)} %maximum_select_fusion.2), channel_id=1, source_target_pairs={{0,4},{1,5},{2,6},{3,7},{4,0},{5,1},{6,2},{7,3},{8,12},{9,13},{10,... | collective-permute-start | bytes 3145736 | tf_op jit(solution)/shard_map/ppermute | solution.py:18
  126.2 47.2 %copy-start.9 = (bf16[1,256,256]{2,1,0:T(8,128)(2,1)S(1)}, bf16[1,256,256]{2,1,0:T(8,128)(2,1)}, u32[]{:S(2)}) copy-start(bf16[1,256,256]{2,1,0:T(8,128)(2,1)} %param.8) | copy-start | bytes 393220
  176.1 0.9 copy-start.5
  176.1 133.6 %all-gather.13.cloned.1.call-start = ((), (), s32[]{:S(2)}) async-start(), calls=%async_computation.12 | async-start | bytes 3342336 | tf_op jit(solution)/shard_map/all_gather | solution.py:70
  176.7 215.6 %reduce-scatter.8.cloned.1.call-start = ((), (), s32[]{:S(2)}) async-start(), calls=%async_computation.6 | async-start | bytes 2228224 | tf_op jit(solution)/shard_map/reduce_scatter | solution.py:94
  179.4 0.8 copy-start.10
  179.4 269.2 %all-gather.15.cloned.1.call-start = ((), (), s32[]{:S(2)}) async-start(), calls=%async_computation.13 | async-start | bytes 3899392 | tf_op jit(solution)/shard_map/all_gather | solution.py:70
  180.0 349.4 %reduce-scatter.10.cloned.1.call-start = ((), (), s32[]{:S(2)}) async-start(), calls=%async_computation.7 | async-start | bytes 1114112 | tf_op jit(solution)/shard_map/reduce_scatter | solution.py:101
  256.0 1.4 collective-permute-start.3
  257.5 8.4 %collective-permute-start.4 = (f32[128,512]{0,1:T(8,128)S(1)}, f32[128,512]{0,1:T(8,128)S(1)}, u32[]{:S(2)}, u32[]{:S(2)}) collective-permute-start(f32[128,512]{0,1:T(8,128)S(1)} %maximum_select_fusion.9), channel_id=1, source_target_pairs={{0,2},{1,3},{2,0},{3,1},{4,6},{5,7},{6,4},{7,5},{8,10},{9,11},{10,... | collective-permute-start | bytes 786440 | tf_op jit(solution)/shard_map/ppermute | solution.py:18
  266.0 48.7 %collective-permute-start.5 = (f32[128,1024]{0,1:T(8,128)S(1)}, f32[128,1024]{0,1:T(8,128)}, u32[]{:S(2)}, u32[]{:S(2)}) collective-permute-start(f32[128,1024]{0,1:T(8,128)S(1)} %maximum_select_fusion.8), channel_id=1, source_target_pairs={{0,4},{1,5},{2,6},{3,7},{4,0},{5,1},{6,2},{7,3},{8,12},{9,13},{10,... | collective-permute-start | bytes 1572872 | tf_op jit(solution)/shard_map/ppermute | solution.py:18
  311.4 2.5 copy-start.1
  396.4 22.0 %copy-start.3 = (f32[384,256]{1,0:T(8,128)}, f32[384,256]{1,0:T(8,128)S(1)}, u32[]{:S(2)}) copy-start(f32[384,256]{1,0:T(8,128)S(1)} %fusion.24) | copy-start | bytes 1179652
  396.5 1.8 collective-permute-start.6
  398.3 19.9 %collective-permute-start.7 = (f32[384,512]{1,0:T(8,128)S(1)}, f32[384,512]{1,0:T(8,128)S(1)}, u32[]{:S(2)}, u32[]{:S(2)}) collective-permute-start(f32[384,512]{1,0:T(8,128)S(1)} %maximum_select_fusion.6), channel_id=1, source_target_pairs={{0,2},{1,3},{2,0},{3,1},{4,6},{5,7},{6,4},{7,5},{8,10},{9,11},{10,... | collective-permute-start | bytes 2359304 | tf_op jit(solution)/shard_map/ppermute | solution.py:18
  418.5 1.2 copy-start
  419.7 2.5 copy-start.6
  422.1 191.5 %reduce-scatter.12.cloned.1.call-start = ((), (), s32[]{:S(2)}) async-start(), calls=%async_computation.8 | async-start | bytes 3342336 | tf_op jit(solution)/shard_map/reduce_scatter | solution.py:94
  427.6 2.5 copy-start.2
  432.2 264.6 %reduce-scatter.14.cloned.1.call-start = ((), (), s32[]{:S(2)}) async-start(), calls=%async_computation.9 | async-start | bytes 557056 | tf_op jit(solution)/shard_map/reduce_scatter | solution.py:101
  448.6 80.8 %copy-start.11 = (bf16[1,64,256]{2,1,0:T(8,128)(2,1)S(1)}, bf16[1,64,256]{2,1,0:T(8,128)(2,1)}, u32[]{:S(2)}) copy-start(bf16[1,64,256]{2,1,0:T(8,128)(2,1)} %param.11) | copy-start | bytes 98308
  530.2 6.1 collective-permute-start.8
  533.9 4.2 copy-start.8
  536.4 6.0 collective-permute-start.9
  541.4 76.7 %copy-start.7 = (bf16[1,448,256]{2,1,0:T(8,128)(2,1)S(1)}, bf16[1,448,256]{2,1,0:T(8,128)(2,1)}, u32[]{:S(2)}) copy-start(bf16[1,448,256]{2,1,0:T(8,128)(2,1)} %param.12) | copy-start | bytes 688132
  616.2 4.7 copy-start.4
  616.2 80.5 %copy-start.12 = (bf16[1,32,256]{2,1,0:T(8,128)(2,1)S(1)}, bf16[1,32,256]{2,1,0:T(8,128)(2,1)}, u32[]{:S(2)}) copy-start(bf16[1,32,256]{2,1,0:T(8,128)(2,1)} %param.13) | copy-start | bytes 49156
  616.2 1.9 collective-permute-start.10
Sparse Core Ops, SparseCore 0:
  9.8 43.6 all-gather.8
  55.9 48.7 all-gather.10
  176.2 78.8 reduce-scatter.5
  257.7 51.9 all-gather.12
  313.5 78.7 reduce-scatter.7
  394.6 53.9 all-gather.14
  452.1 77.2 reduce-scatter.9
  533.4 80.1 reduce-scatter.11
  620.1 76.6 reduce-scatter.13
where the time goes:
time: 706 us; the launch traced here: 705 us
  waiting for transfers between devices  620 us (88%)
  matrix products  31.8 us (5%)
  local copies, waits for them, and re-layouts  15.5 us (2%)
  between operations  14.1 us (2%)
  starting transfers between devices  12.7 us (2%)
  other arithmetic  10.9 us (2%)
    reduce_scatter x3, waiting for transfers between devices, per_device(): lax.psum_scatter(diag_terms, 'row', scatter_dimension=0, tiled=True)  227 us
    reduce_scatter x2, waiting for transfers between devices, per_device(): reduced = lax.psum_scatter(joined, 'row', scatter_dimension=0, tiled=True)  147 us
    all_gather x3, waiting for transfers between devices, per_device(): gathered = lax.all_gather(factor_tile, 'row', axis=0, tiled=True)  109 us
    ppermute x11, waiting for transfers between devices, swapped(): return lax.ppermute(value, axis, pairs)  89.8 us
    all_gather x1, waiting for transfers between devices, per_device(): root_rows = lax.all_gather(root_block[0], 'col', axis=1, tiled=True)  44.7 us
    dot_general x6, matrix products, transposed_product(): lax.dot_general(left_side, right_side, (((0,), (0,)), ((), ())), precisio...  14.2 us
  transfers between devices with their start and end apart: 20, of which 18 were waited for; matrix products, arithmetic and copies ran while one was open for 6% of the time, Pallas kernels for 0%

commit v1 on v0

v1 whole, which is shorter than its diff:
```python
import jax
import jax.numpy as jnp
from jax import lax
from jax.experimental import pallas as pl
from jax.experimental.pallas import tpu as pltpu
from jax.sharding import PartitionSpec as P

MESH = pl.DeviceIdType.MESH
F32 = jnp.float32
BF16 = jnp.bfloat16


def wrap(value, extent):
    return lax.rem(value + extent, extent)


def remote(src, dst, send_sem, recv_sem, device):
    return pltpu.make_async_remote_copy(
        src_ref=src, dst_ref=dst, send_sem=send_sem, recv_sem=recv_sem,
        device_id=device, device_id_type=MESH,
    )


def halves(value):
    high = value.astype(BF16)
    low = (value - high.astype(F32)).astype(BF16)
    return high, low


def product(left_tiles, right_tiles):
    left = jnp.concatenate(left_tiles, 1) if len(left_tiles) > 1 else left_tiles[0]
    right = jnp.concatenate(right_tiles, 0) if len(right_tiles) > 1 else right_tiles[0]
    return jnp.dot(left, right, preferred_element_type=F32)


def folded(value):
    rows = value.shape[0] // 2
    return value[:rows] + value[rows:]


class Plane:
    def __init__(self, source, held, send, recv, local, at):
        self.source, self.held, self.send, self.recv, self.local = source, held, send, recv, local
        self.x, self.y, self.c = at
        self.rows = source.shape[0]
        self.half = self.rows // 2
        self.quarter = self.half // 2
        self.started = []

    def device(self, x, y):
        return (wrap(x, 4) * 4 + wrap(y, 4), self.c)

    def targets(self, first):
        x, y = self.x, self.y
        along_x = [self.device(x + 1, y), self.device(x - 1, y)]
        along_y = [self.device(x, y + 1), self.device(x, y - 1)]
        return along_x + along_y if first else along_y + along_x

    def go(self, stage, lane, src, dst, device):
        copy = remote(src, dst, self.send.at[stage, lane], self.recv.at[stage, lane], device)
        copy.start()
        self.started.append(copy)

    def arrive(self, stage, lane, dst):
        remote(dst, dst, self.send.at[stage, lane], self.recv.at[stage, lane], self.device(self.x, self.y + 1)).wait_recv()

    def near(self, lane):
        x, y, held, half, rows = self.x, self.y, self.held, self.half, self.rows
        return [
            held.at[wrap(x - 1, 4), y, 0:half],
            held.at[wrap(x + 1, 4), y, 0:half],
            held.at[x, wrap(y - 1, 4), half:rows],
            held.at[x, wrap(y + 1, 4), half:rows],
        ][lane]

    def open(self):
        self.own = pltpu.make_async_copy(self.source, self.held.at[self.x, self.y], self.local)
        for lane, device in enumerate(self.targets(True)):
            part = slice(0, self.half) if lane < 2 else slice(self.half, self.rows)
            self.go(0, lane, self.source.at[part], self.held.at[self.x, self.y, part], device)
        self.own.start()

    def cross(self):
        x, y, held, half, quarter, rows = self.x, self.y, self.held, self.half, self.quarter, self.rows
        parts = [
            held.at[wrap(x - 1, 4), y, 0:quarter],
            held.at[wrap(x + 1, 4), y, quarter:half],
            held.at[x, wrap(y - 1, 4), half:half + quarter],
            held.at[x, wrap(y + 1, 4), half + quarter:rows],
        ]
        for lane, device in enumerate(self.targets(True)):
            self.arrive(0, lane, self.near(lane))
            self.go(1, lane, parts[lane], parts[lane], device)

    def spread(self):
        x, y, held, half, quarter, rows = self.x, self.y, self.held, self.half, self.quarter, self.rows
        far_x, far_y = wrap(x + 2, 4), wrap(y + 2, 4)
        for lane, part in enumerate([
            held.at[far_x, y, 0:quarter],
            held.at[far_x, y, quarter:half],
            held.at[x, far_y, half:half + quarter],
            held.at[x, far_y, half + quarter:rows],
        ]):
            self.arrive(1, lane, part)
        self.own.wait()
        line_x, line_y = held.at[:, y, 0:half], held.at[x, :, half:rows]
        for lane, device in enumerate(self.targets(False)):
            part = line_x if lane < 2 else line_y
            self.go(2, lane, part, part, device)

    def close(self):
        x, y, held, half, rows = self.x, self.y, self.held, self.half, self.rows
        whole = [
            held.at[:, wrap(y - 1, 4), 0:half],
            held.at[:, wrap(y + 1, 4), 0:half],
            held.at[wrap(x - 1, 4), :, half:rows],
            held.at[wrap(x + 1, 4), :, half:rows],
        ]
        parts = [
            held.at[0:2, wrap(y - 1, 4), 0:half],
            held.at[2:4, wrap(y + 1, 4), 0:half],
            held.at[wrap(x - 1, 4), 0:2, half:rows],
            held.at[wrap(x + 1, 4), 2:4, half:rows],
        ]
        for lane, device in enumerate(self.targets(False)):
            self.arrive(2, lane, whole[lane])
            self.go(3, lane, parts[lane], parts[lane], device)

    def finish(self):
        x, y, held, half, rows = self.x, self.y, self.held, self.half, self.rows
        far_x, far_y = wrap(x + 2, 4), wrap(y + 2, 4)
        for lane, part in enumerate([
            held.at[0:2, far_y, 0:half],
            held.at[2:4, far_y, 0:half],
            held.at[far_x, 0:2, half:rows],
            held.at[far_x, 2:4, half:rows],
        ]):
            self.arrive(3, lane, part)

    def block(self, start, width, tile):
        per_tile = 256 // width
        found = []
        for piece in range(per_tile):
            run = tile * per_tile + piece
            found.append(self.held[run // 4, run % 4, start:start + width])
        return found


class Ring:
    def __init__(self, source, held, send, recv, partner_send, partner_recv, local, at):
        self.source, self.held, self.send, self.recv = source, held, send, recv
        self.partner_send, self.partner_recv, self.local = partner_send, partner_recv, local
        self.r, self.z, self.core = at
        self.started = []

    def slot(self, z, core):
        return self.held.at[wrap(z, 8) * 2 + core, 0:256]

    def device(self, z, core):
        return (self.r, wrap(z, 8) * 2 + core)

    def go(self, step, lane, src, dst):
        shift = 1 if lane == 0 else -1
        copy = remote(src, dst, self.send.at[step, lane], self.recv.at[step, lane], self.device(self.z + shift, self.core))
        copy.start()
        self.started.append(copy)

    def share(self, index, src, dst):
        copy = remote(src, dst, self.partner_send.at[index], self.partner_recv.at[index], self.device(self.z, 1 - self.core))
        copy.start()
        self.started.append(copy)

    def arrive(self, step, lane, dst):
        remote(dst, dst, self.send.at[step, lane], self.recv.at[step, lane], self.device(self.z + 1, self.core)).wait_recv()

    def open(self):
        own = self.slot(self.z, self.core)
        for lane in range(2):
            self.go(0, lane, self.source, own)
        self.share(0, self.source, own)
        self.own = pltpu.make_async_copy(self.source, own, self.local)
        self.own.start()

    def step(self, number):
        for lane in range(2):
            distance = -number if lane == 0 else number
            tile = self.slot(self.z + distance, self.core)
            self.arrive(number - 1, lane, tile)
            if number < 3:
                self.go(number, lane, tile, tile)
            else:
                part = self.held.at[wrap(self.z + distance, 8) * 2 + self.core, 128 * lane:128 * lane + 128]
                self.go(number, lane, part, part)
            self.share(2 * number - 1 + lane, tile, tile)

    def finish(self):
        far = wrap(self.z + 4, 8) * 2 + self.core
        for lane in range(2):
            self.arrive(3, lane, self.held.at[far, 128 * lane:128 * lane + 128])
        tile = self.slot(self.z + 4, self.core)
        self.share(7, tile, tile)
        other = 1 - self.core
        for index, distance in enumerate([0, -1, 1, -2, 2, -3, 3, 4]):
            tile = self.slot(self.z + distance, other)
            remote(tile, tile, self.partner_send.at[index], self.partner_recv.at[index], self.device(self.z, other)).wait_recv()
        self.own.wait()


class Node:
    def __init__(self, held, rows, chips, send, recv, partner_send, partner_recv, at):
        self.held, self.rows, self.chips = held, rows, chips
        self.send, self.recv, self.partner_send, self.partner_recv = send, recv, partner_send, partner_recv
        self.r, self.z, self.core = at
        self.first = self.z - lax.rem(self.z, chips)
        self.place = lax.rem(self.z, chips)
        self.started = []

    def slot(self, place, core):
        return self.held.at[place * 2 + core, self.rows]

    def share(self, index, tile):
        copy = remote(tile, tile, self.partner_send.at[index], self.partner_recv.at[index],
                      (self.r, self.z * 2 + 1 - self.core))
        copy.start()
        self.started.append(copy)

    def open(self):
        tile = self.slot(self.place, self.core)
        for hop in range(1, self.chips):
            target = wrap(self.place + hop, self.chips)
            copy = remote(tile, tile, self.send.at[hop], self.recv.at[hop], (self.r, (self.first + target) * 2 + self.core))
            copy.start()
            self.started.append(copy)
        self.share(0, tile)

    def relay(self):
        for hop in range(1, self.chips):
            tile = self.slot(wrap(self.place - hop, self.chips), self.core)
            remote(tile, tile, self.send.at[hop], self.recv.at[hop], (self.r, self.z * 2 + 1 - self.core)).wait_recv()
            self.share(hop, tile)

    def finish(self):
        other = 1 - self.core
        for hop in range(self.chips):
            tile = self.slot(wrap(self.place - hop, self.chips), other)
            remote(tile, tile, self.partner_send.at[hop], self.partner_recv.at[hop], (self.r, self.z * 2 + other)).wait_recv()


class Turn:
    def __init__(self, source, place, whole, send, recv, partner_send, partner_recv, local, at):
        self.source, self.place, self.whole = source, place, whole
        self.send, self.recv, self.partner_send, self.partner_recv, self.local = send, recv, partner_send, partner_recv, local
        self.r, self.c, self.core = at
        self.started = []

    def open(self):
        self.own = pltpu.make_async_copy(self.source.at[self.r], self.place(self.r, self.core), self.local)
        self.own.start()
        for hop in range(1, 16):
            target = wrap(self.r + hop, 16)
            copy = remote(self.source.at[target], self.place(self.r, self.core), self.send.at[hop], self.recv.at[hop], (target, self.c))
            copy.start()
            self.started.append(copy)

    def relay(self):
        for hop in range(1, 16):
            part = self.place(wrap(self.r - hop, 16), self.core)
            remote(part, part, self.send.at[hop], self.recv.at[hop], (wrap(self.r + 1, 16), self.c)).wait_recv()
        self.own.wait()
        part = self.whole(self.core)
        copy = remote(part, part, self.partner_send, self.partner_recv, (self.r, self.c + 1 - 2 * self.core))
        copy.start()
        self.started.append(copy)

    def finish(self):
        part = self.whole(1 - self.core)
        remote(part, part, self.partner_send, self.partner_recv, (self.r, self.c + 1 - 2 * self.core)).wait_recv()


def kernel(root, l_one, l_two, l_three, d_one, d_two, d_three, out_one, out_two, out_three,
           p_zero, p_one, p_two, p_three, g_one, g_two, g_three, turn_one, turn_two, turn_cross, sums, gained,
           plane_send, plane_recv, ring_send, ring_recv, ring_core_send, ring_core_recv,
           node_send, node_recv, node_core_send, node_core_recv,
           turn_send, turn_recv, turn_core_send, turn_core_recv, last_send, last_recv, local):
    r, c = lax.axis_index("row"), lax.axis_index("col")
    x, y = lax.div(r, 4), lax.rem(r, 4)
    z, core = lax.div(c, 2), lax.rem(c, 2)
    eighth, quarter = lax.rem(c, 8), lax.rem(c, 4)

    barrier = pltpu.get_barrier_semaphore()
    for hop in range(1, 16):
        pl.semaphore_signal(barrier, inc=1, device_id=(wrap(r + hop, 16), c), device_id_type=MESH)
    for hop in range(1, 8):
        pl.semaphore_signal(barrier, inc=1, device_id=(r, wrap(z + hop, 8) * 2 + core), device_id_type=MESH)
    pl.semaphore_signal(barrier, inc=1, device_id=(r, z * 2 + 1 - core), device_id_type=MESH)
    pl.semaphore_wait(barrier, 23)

    planes = [
        Plane(source, held, plane_send.at[level], plane_recv.at[level], local.at[level], (x, y, c))
        for level, (source, held) in enumerate([(l_one, g_one), (l_two, g_two), (l_three, g_three)])
    ]
    one, two, three = planes
    ring = Ring(root, p_zero, ring_send, ring_recv, ring_core_send, ring_core_recv, local.at[3], (r, z, core))

    def node(index, held, rows, chips):
        return Node(held, rows, chips, node_send.at[index], node_recv.at[index], node_core_send.at[index],
                    node_core_recv.at[index], (r, z, core))

    s01 = node(0, p_one, slice(0, 512), 4)
    s11 = node(1, p_one, slice(512, 768), 4)
    s02 = node(2, p_two, slice(0, 512), 2)
    s12 = node(3, p_two, slice(512, 768), 2)
    s22 = node(4, p_two, slice(768, 896), 2)

    def turn(index, source, place, whole):
        return Turn(source, place, whole, turn_send.at[index], turn_recv.at[index], turn_core_send.at[index],
                    turn_core_recv.at[index], local.at[4 + index], (r, c, core))

    def rows_at(start, size, which):
        return pl.ds(pl.multiple_of(start + size * which, size), size)

    t01 = turn(0, turn_one, lambda run, which: p_zero.at[run, rows_at(256, 128, which)],
               lambda which: p_zero.at[:, rows_at(256, 128, which)])
    t02 = turn(1, turn_two, lambda run, which: p_zero.at[run, rows_at(512, 64, which)],
               lambda which: p_zero.at[:, rows_at(512, 64, which)])
    t12 = turn(2, turn_cross,
               lambda run, which: p_one.at[lax.div(run, 2), rows_at(768, 64, which),
                                           pl.ds(pl.multiple_of(lax.rem(run, 2) * 128, 128), 128)],
               lambda which: p_one.at[:, rows_at(768, 64, which)])

    def store(held, index, start, value):
        rows = value.shape[0]
        high, low = halves(value)
        held[index, start:start + rows] = high
        held[index, start + rows:start + 2 * rows] = low

    def zero_part(plane, first, last):
        return product([p_zero[k, first:last] for k in range(16)],
                       [piece for k in range(16) for piece in plane.block(0, 256, k)])

    def one_part(plane, first, last):
        return product([p_one[k, first:last] for k in range(8)],
                       [piece for k in range(8) for piece in plane.block(256, 128, k)])

    def two_part(plane, first, last):
        return product([p_two[k, first:last] for k in range(4)],
                       [piece for k in range(4) for piece in plane.block(384, 64, k)])

    one.open()
    ring.open()
    two.open()
    one.cross()
    ring.step(1)
    one.spread()
    ring.step(2)
    two.cross()
    three.open()
    one.close()
    ring.step(3)
    two.spread()
    three.cross()
    one.finish()
    ring.finish()

    value = -zero_part(one, 0, 256)
    store(p_one, eighth, 0, value)
    s01.open()
    out_one[0, 0:256] = value

    two.close()
    three.spread()
    s01.relay()
    s01.finish()
    for k in range(8):
        tile = p_one[k, rows_at(0, 256, core)]
        turned = tile.T
        turn_one[2 * k] = turned[0:128]
        turn_one[2 * k + 1] = turned[128:256]
    t01.open()

    two.finish()
    value = -(zero_part(two, 0, 256) + folded(one_part(two, 0, 512)))
    store(p_two, quarter, 0, value)
    s02.open()
    out_two[0, 0:256] = value

    t01.relay()
    t01.finish()
    value = d_one[...].astype(F32) - folded(zero_part(one, 256, 512))
    store(p_one, eighth, 512, value)
    s11.open()
    out_one[0, 256:384] = value

    three.close()
    s02.relay()
    s02.finish()
    for k in range(4):
        tile = p_two[k, rows_at(0, 256, core)]
        turned = tile.T
        for piece in range(4):
            turn_two[4 * k + piece] = turned[64 * piece:64 * piece + 64]
    t02.open()

    s11.relay()
    s11.finish()
    value = -folded(zero_part(two, 256, 512) + one_part(two, 512, 768))
    store(p_two, quarter, 512, value)
    s12.open()
    out_two[0, 256:384] = value

    s12.relay()
    s12.finish()
    for k in range(4):
        tile = p_two[k, rows_at(512, 128, core)]
        turned = tile.T
        for piece in range(4):
            turn_cross[4 * k + piece] = turned[64 * piece:64 * piece + 64]
    t12.open()

    three.finish()
    upper = -(zero_part(three, 0, 256) + folded(one_part(three, 0, 512)) + folded(two_part(three, 0, 512)))
    out_three[0, 0:256] = upper
    high, low = halves(upper)
    p_three[core, 0:256] = high
    p_three[core, 448:704] = low
    middle = -folded(zero_part(three, 256, 512) + one_part(three, 512, 768) + two_part(three, 512, 768))
    out_three[0, 256:384] = middle
    high, low = halves(middle)
    p_three[core, 256:384] = high
    p_three[core, 704:832] = low

    t02.relay()
    t12.relay()
    t02.finish()
    t12.finish()
    value = d_two[...].astype(F32) - folded(zero_part(two, 512, 640) + one_part(two, 768, 896))
    store(p_two, quarter, 768, value)
    s22.open()
    out_two[0, 384:448] = value
    s22.relay()
    s22.finish()

    lower = -folded(zero_part(three, 512, 640) + one_part(three, 768, 896) + two_part(three, 768, 896))
    out_three[0, 384:448] = lower
    high, low = halves(lower)
    p_three[core, 384:448] = high
    p_three[core, 832:896] = low
    mine = p_three.at[core]
    swap = remote(mine, mine, last_send.at[0], last_recv.at[0], (r, z * 2 + 1 - core))
    swap.start()
    theirs = p_three.at[1 - core]
    remote(theirs, theirs, last_send.at[0], last_recv.at[0], (r, z * 2 + 1 - core)).wait_recv()
    factor = l_three[...]
    for which in range(2):
        turned = jnp.concatenate([p_three[which, 0:448].T, p_three[which, 448:896].T], 0)
        partial = folded(jnp.dot(turned, factor, preferred_element_type=F32))
        for piece in range(8):
            sums[8 * which + piece] = partial[32 * piece:32 * piece + 32]
    final = []
    for hop in range(1, 16):
        target = wrap(r + hop, 16)
        copy = remote(sums.at[target], gained.at[r], last_send.at[hop], last_recv.at[hop], (target, c))
        copy.start()
        final.append(copy)
    total = sums[r]
    for hop in range(1, 16):
        source = wrap(r - hop, 16)
        part = gained.at[source]
        remote(part, part, last_send.at[hop], last_recv.at[hop], (wrap(r + 1, 16), c)).wait_recv()
        total = total + gained[source]
    out_three[0, 448:480] = d_three[...].astype(F32) - total

    swap.wait_send()
    for group in [one, two, three, ring, s01, s11, s02, s12, s22, t01, t02, t12]:
        for copy in group.started:
            copy.wait_send()
    for copy in final:
        copy.wait_send()


def per_device(root_block, l_one, dinv_one, l_two, dinv_two, l_three, dinv_three):
    vmem = pl.BlockSpec(memory_space=pltpu.VMEM)
    dma = pltpu.SemaphoreType.DMA
    return pl.pallas_call(
        kernel,
        out_shape=(
            jax.ShapeDtypeStruct((1, 384, 256), F32),
            jax.ShapeDtypeStruct((1, 448, 256), F32),
            jax.ShapeDtypeStruct((1, 480, 256), F32),
        ),
        in_specs=[vmem] * 7,
        out_specs=(vmem, vmem, vmem),
        scratch_shapes=[
            pltpu.VMEM((16, 640, 256), BF16),
            pltpu.VMEM((8, 896, 256), BF16),
            pltpu.VMEM((4, 896, 256), BF16),
            pltpu.VMEM((2, 896, 256), BF16),
            pltpu.VMEM((4, 4, 256, 256), BF16),
            pltpu.VMEM((4, 4, 384, 256), BF16),
            pltpu.VMEM((4, 4, 448, 256), BF16),
            pltpu.VMEM((16, 128, 256), BF16),
            pltpu.VMEM((16, 64, 256), BF16),
            pltpu.VMEM((16, 64, 128), BF16),
            pltpu.VMEM((16, 32, 256), F32),
            pltpu.VMEM((16, 32, 256), F32),
            dma((3, 4, 4)), dma((3, 4, 4)),
            dma((4, 2)), dma((4, 2)), dma((8,)), dma((8,)),
            dma((5, 4)), dma((5, 4)), dma((5, 4)), dma((5, 4)),
            dma((3, 16)), dma((3, 16)), dma((3,)), dma((3,)),
            dma((16,)), dma((16,)),
            dma((7,)),
        ],
        compiler_params=pltpu.CompilerParams(
            collective_id=0, has_side_effects=True, vmem_limit_bytes=60 * 1024 * 1024
        ),
    )(root_block[0], l_one[0], l_two[0], l_three[0], dinv_one[0], dinv_two[0], dinv_three[0])


def solution(mesh):
    placed = (P("row", None, "col"),) * 7
    return jax.shard_map(
        per_device,
        mesh=mesh,
        in_specs=placed,
        out_specs=(P("row", None, "col"), P("row", None, "col"), P("row", None, "col")),
        check_vma=False,
    )
```

time: 706 us -> 137 us (0.19)
  waiting for transfers between devices: 620 us -> 0 us
  Pallas kernels: 0 us -> 130 us
  matrix products: 31.8 us -> 0 us
  between operations: 14.1 us -> 0.65 us
  starting transfers between devices: 12.7 us -> 0 us
  local copies, waits for them, and re-layouts: 15.5 us -> 3.8 us
  other arithmetic: 10.9 us -> 0 us
    reduce_scatter x5 -> x0, waiting for transfers between devices: 374 us -> none  [the longest x3 227 us: per_device(): lax.psum_scatter(diag_terms, 'row', scatter_dimension=0, tiled=True)]
    all_gather x4 -> x0, waiting for transfers between devices: 153 us -> none  [the longest x3 109 us: per_device(): gathered = lax.all_gather(factor_tile, 'row', axis=0, tiled=True)]
    pallas_call x0 -> x1, Pallas kernels: none -> 130 us  [per_device(): pl.pallas_call(kernel, out_shape=(jax.ShapeDtypeStruct((1, 384, 256), F32...]
    ppermute x11 -> x0, waiting for transfers between devices: 89.8 us -> none  [swapped(): return lax.ppermute(value, axis, pairs)]
    dot_general x12 -> x0, matrix products: 31.8 us -> none  [the longest x6 14.2 us: transposed_product(): lax.dot_general(left_side, right_side, (((0,), (0,)), ((), ())), precisio...]
    ppermute x11 -> x0, starting transfers between devices: 12.4 us -> none  [swapped(): return lax.ppermute(value, axis, pairs)]
    slice x5 -> x0, local copies, waits for them, and re-layouts: 9.73 us -> none  [per_device(): stacked[:, row_offsets[block_index]:row_offsets[block_index + 1], :]]
  transfers between devices with their start and end apart: 20 -> 0, of which waited for: 18 -> 0; matrix products, arithmetic and copies ran while one was open for 6% -> 0% of each run, Pallas kernels for 0% -> 0%
where the time goes in v1:
time: 137 us; the launch traced here: 135 us
  Pallas kernels  130 us (95%)
  local copies, waits for them, and re-layouts  3.8 us (3%)
    pallas_call x1, Pallas kernels, per_device(): pl.pallas_call(kernel, out_shape=(jax.ShapeDtypeStruct((1, 384, 256), F32...  130 us
    unnamed x7, local copies, waits for them, and re-layouts  3.8 us

profile of v1, /device:TPU:24, one launch (start us, length us, event | category | flops | bytes accessed | tf_op | source)
XLA Modules:
  0.0 134.9 jit_solution(1366086497723705453)
XLA Ops:
  0.6 130.4 %shard_map.94 = (f32[1,384,256]{2,1,0:T(8,128)}, f32[1,448,256]{2,1,0:T(8,128)}, f32[1,480,256]{2,1,0:T(8,128)}) custom-call(bf16[256,256]{1,0:T(8,128)(2,1)} %bitcast.9, bf16[256,256]{1,0:T(8,128)(2,1)} %bitcast.10, bf16[384,256]{1,0:T(8,128)(2,1)} %bitcast.8, bf16[448,256]{1,0:T(8,128)(2,1)} %bitcast.7, bf16[128,256]{1,0:T(8,128)(2,1)} %bitcast.11, ...), custom_call_target="tpu_custom_call" | custom-call | tf_op jit(solution)/shard_map/pallas_call | solution.py:484
  131.1 0.0 copy-start.1
  131.1 1.8 %copy.13 = f32[1,384,256]{2,1,0:T(8,128)} copy(f32[1,384,256]{2,1,0:T(8,128)} %get-tuple-element.6) | data formatting | bytes 786432
  132.9 0.0 copy-done.1
  132.9 0.0 copy-start
  132.9 0.8 copy.14
  133.7 0.4 copy-done
  134.1 0.8 copy.15
Async XLA Ops:
  131.1 1.8 %copy-start.1 = (f32[1,448,256]{2,1,0:T(8,128)S(1)}, f32[1,448,256]{2,1,0:T(8,128)}, u32[]{:S(2)}) copy-start(f32[1,448,256]{2,1,0:T(8,128)} %get-tuple-element.7) | copy-start | bytes 1376260
  132.9 1.2 copy-start

commit v2 on v1

--- a/solution.py
+++ b/solution.py
@@ -36,6 +36,11 @@
 def folded(value):
     rows = value.shape[0] // 2
     return value[:rows] + value[rows:]
+
+
+def folded_halves(value):
+    rows = value.shape[0] // 2
+    return jnp.concatenate([folded(value[:rows]), folded(value[rows:])], 0)
 
 
 class Plane:
@@ -246,6 +251,69 @@
             remote(tile, tile, self.partner_send.at[hop], self.partner_recv.at[hop], (self.r, self.z * 2 + other)).wait_recv()
 
 
+class Chain:
+    def __init__(self, held, rows, send, recv, partner_send, partner_recv, at):
+        self.held, self.rows = held, rows
+        self.send, self.recv, self.partner_send, self.partner_recv = send, recv, partner_send, partner_recv
+        self.r, self.z, self.core = at
+        self.first = self.z - lax.rem(self.z, 4)
+        place = lax.rem(self.z, 4)
+        upper, odd = lax.div(place, 2), lax.rem(place, 2)
+        self.beside, self.across = place + 1 - 2 * odd, 3 - place
+        self.inner = (upper + odd) == 1
+        self.order = [place, self.beside, 2 - upper, 3 - 3 * upper]
+        self.started, self.started_inner = [], []
+
+    def slot(self, place, core):
+        return self.held.at[place * 2 + core, self.rows]
+
+    def copy(self, index, lane, place, target):
+        tile = self.slot(place, self.core)
+        return remote(tile, tile, self.send.at[index], self.recv.at[lane], (self.r, (self.first + target) * 2 + self.core))
+
+    def share(self, index):
+        tile = self.slot(self.order[index], self.core)
+        copy = remote(tile, tile, self.partner_send.at[index], self.partner_recv.at[index],
+                      (self.r, self.z * 2 + 1 - self.core))
+        copy.start()
+        self.started.append(copy)
+
+    def inward(self, copy):
+        self.started_inner.append(copy)
+
+        @pl.when(self.inner)
+        def _():
+            copy.start()
+
+    def open(self):
+        self.inward(self.copy(1, 1, self.order[0], self.across))
+        copy = self.copy(0, 0, self.order[0], self.beside)
+        copy.start()
+        self.started.append(copy)
+        self.share(0)
+
+    def relay(self):
+        targets = [self.across, self.beside, self.beside]
+        lanes = [2, 1, 2]
+        for lane in range(3):
+            tile = self.slot(self.order[lane + 1], self.core)
+            remote(tile, tile, self.send.at[0], self.recv.at[lane], (self.r, self.z * 2 + 1 - self.core)).wait_recv()
+            self.inward(self.copy(2 + lane, lanes[lane], self.order[lane + 1], targets[lane]))
+            self.share(lane + 1)
+
+    def finish(self):
+        other = 1 - self.core
+        for index in range(4):
+            tile = self.slot(self.order[index], other)
+            remote(tile, tile, self.partner_send.at[index], self.partner_recv.at[index], (self.r, self.z * 2 + other)).wait_recv()
+
+    def drain(self):
+        @pl.when(self.inner)
+        def _():
+            for copy in self.started_inner:
+                copy.wait_send()
+
+
 class Turn:
     def __init__(self, source, place, whole, send, recv, partner_send, partner_recv, local, at):
         self.source, self.place, self.whole = source, place, whole
@@ -281,6 +349,7 @@
            p_zero, p_one, p_two, p_three, g_one, g_two, g_three, turn_one, turn_two, turn_cross, sums, gained,
            plane_send, plane_recv, ring_send, ring_recv, ring_core_send, ring_core_recv,
            node_send, node_recv, node_core_send, node_core_recv,
+           chain_send, chain_recv, chain_core_send, chain_core_recv, swap_send, swap_recv,
            turn_send, turn_recv, turn_core_send, turn_core_recv, last_send, last_recv, local):
     r, c = lax.axis_index("row"), lax.axis_index("col")
     x, y = lax.div(r, 4), lax.rem(r, 4)
@@ -306,11 +375,15 @@
         return Node(held, rows, chips, node_send.at[index], node_recv.at[index], node_core_send.at[index],
                     node_core_recv.at[index], (r, z, core))
 
-    s01 = node(0, p_one, slice(0, 512), 4)
-    s11 = node(1, p_one, slice(512, 768), 4)
-    s02 = node(2, p_two, slice(0, 512), 2)
-    s12 = node(3, p_two, slice(512, 768), 2)
-    s22 = node(4, p_two, slice(768, 896), 2)
+    def chain(index, held, rows):
+        return Chain(held, rows, chain_send.at[index], chain_recv.at[index], chain_core_send.at[index],
+                     chain_core_recv.at[index], (r, z, core))
+
+    s01 = [chain(0, p_one, slice(0, 256)), chain(1, p_one, slice(256, 512))]
+    s11 = chain(2, p_one, slice(512, 768))
+    s02 = node(0, p_two, slice(0, 512), 2)
+    s12 = node(1, p_two, slice(512, 768), 2)
+    s22 = node(2, p_two, slice(768, 896), 2)
 
     def turn(index, source, place, whole):
         return Turn(source, place, whole, turn_send.at[index], turn_recv.at[index], turn_core_send.at[index],
@@ -319,11 +392,15 @@
     def rows_at(start, size, which):
         return pl.ds(pl.multiple_of(start + size * which, size), size)
 
-    t01 = turn(0, turn_one, lambda run, which: p_zero.at[run, rows_at(256, 128, which)],
-               lambda which: p_zero.at[:, rows_at(256, 128, which)])
-    t02 = turn(1, turn_two, lambda run, which: p_zero.at[run, rows_at(512, 64, which)],
+    def half_turn(half):
+        lanes = slice(128 * half, 128 * half + 128)
+        return turn(2 + half, turn_one.at[half], lambda run, which: p_zero.at[run, rows_at(256, 128, which), lanes],
+                    lambda which: p_zero.at[:, rows_at(256, 128, which), lanes])
+
+    t01 = [half_turn(0), half_turn(1)]
+    t02 = turn(0, turn_two, lambda run, which: p_zero.at[run, rows_at(512, 64, which)],
                lambda which: p_zero.at[:, rows_at(512, 64, which)])
-    t12 = turn(2, turn_cross,
+    t12 = turn(1, turn_cross,
                lambda run, which: p_one.at[lax.div(run, 2), rows_at(768, 64, which),
                                            pl.ds(pl.multiple_of(lax.rem(run, 2) * 128, 128), 128)],
                lambda which: p_one.at[:, rows_at(768, 64, which)])
@@ -348,44 +425,48 @@
 
     one.open()
     ring.open()
-    two.open()
     one.cross()
     ring.step(1)
     one.spread()
+    two.open()
     ring.step(2)
+    one.close()
     two.cross()
     three.open()
-    one.close()
     ring.step(3)
+    one.finish()
     two.spread()
     three.cross()
-    one.finish()
     ring.finish()
 
-    value = -zero_part(one, 0, 256)
-    store(p_one, eighth, 0, value)
-    s01.open()
-    out_one[0, 0:256] = value
+    for half in range(2):
+        value = -zero_part(one, 128 * half, 128 * half + 128)
+        store(p_one, eighth, 256 * half, value)
+        s01[half].open()
+        out_one[0, 128 * half:128 * half + 128] = value
 
     two.close()
     three.spread()
-    s01.relay()
-    s01.finish()
-    for k in range(8):
-        tile = p_one[k, rows_at(0, 256, core)]
-        turned = tile.T
-        turn_one[2 * k] = turned[0:128]
-        turn_one[2 * k + 1] = turned[128:256]
-    t01.open()
+    for half in range(2):
+        s01[half].relay()
+        s01[half].finish()
+        for k in range(8):
+            tile = p_one[k, rows_at(256 * half, 128, core)]
+            turned = tile.T
+            turn_one[half, 2 * k] = turned[0:128]
+            turn_one[half, 2 * k + 1] = turned[128:256]
+        t01[half].open()
 
     two.finish()
-    value = -(zero_part(two, 0, 256) + folded(one_part(two, 0, 512)))
+    value = -(zero_part(two, 0, 256) + folded_halves(one_part(two, 0, 512)))
     store(p_two, quarter, 0, value)
     s02.open()
     out_two[0, 0:256] = value
 
-    t01.relay()
-    t01.finish()
+    for half in range(2):
+        t01[half].relay()
+    for half in range(2):
+        t01[half].finish()
     value = d_one[...].astype(F32) - folded(zero_part(one, 256, 512))
     store(p_one, eighth, 512, value)
     s11.open()
@@ -418,16 +499,29 @@
     t12.open()
 
     three.finish()
-    upper = -(zero_part(three, 0, 256) + folded(one_part(three, 0, 512)) + folded(two_part(three, 0, 512)))
+    upper = -(zero_part(three, 0, 256) + folded_halves(one_part(three, 0, 512)) + folded(two_part(three, 0, 512)))
     out_three[0, 0:256] = upper
     high, low = halves(upper)
     p_three[core, 0:256] = high
-    p_three[core, 448:704] = low
+    p_three[core, 384:640] = low
     middle = -folded(zero_part(three, 256, 512) + one_part(three, 512, 768) + two_part(three, 512, 768))
     out_three[0, 256:384] = middle
     high, low = halves(middle)
     p_three[core, 256:384] = high
-    p_three[core, 704:832] = low
+    p_three[core, 640:768] = low
+
+    def swapped(index, rows):
+        mine, theirs = p_three.at[core, rows], p_three.at[1 - core, rows]
+        device = (r, z * 2 + 1 - core)
+        return (remote(mine, mine, swap_send.at[index], swap_recv.at[index], device),
+                remote(theirs, theirs, swap_send.at[index], swap_recv.at[index], device))
+
+    def inner_terms(which, start, size, factor):
+        turned = jnp.concatenate([p_three[which, start:start + size].T, p_three[which, start + size:start + 2 * size].T], 0)
+        return folded(jnp.dot(turned, factor, preferred_element_type=F32))
+
+    first_swap, first_gain = swapped(0, slice(0, 768))
+    first_swap.start()
 
     t02.relay()
     t12.relay()
@@ -437,25 +531,26 @@
     store(p_two, quarter, 768, value)
     s22.open()
     out_two[0, 384:448] = value
+    first_gain.wait_recv()
+    for which in range(2):
+        partial = inner_terms(which, 0, 384, l_three[0:384])
+        for piece in range(8):
+            sums[8 * which + piece] = partial[32 * piece:32 * piece + 32]
     s22.relay()
     s22.finish()
 
     lower = -folded(zero_part(three, 512, 640) + one_part(three, 768, 896) + two_part(three, 768, 896))
+    high, low = halves(lower)
+    p_three[core, 768:832] = high
+    p_three[core, 832:896] = low
+    last_swap, last_gain = swapped(1, slice(768, 896))
+    last_swap.start()
     out_three[0, 384:448] = lower
-    high, low = halves(lower)
-    p_three[core, 384:448] = high
-    p_three[core, 832:896] = low
-    mine = p_three.at[core]
-    swap = remote(mine, mine, last_send.at[0], last_recv.at[0], (r, z * 2 + 1 - core))
-    swap.start()
-    theirs = p_three.at[1 - core]
-    remote(theirs, theirs, last_send.at[0], last_recv.at[0], (r, z * 2 + 1 - core)).wait_recv()
-    factor = l_three[...]
+    last_gain.wait_recv()
     for which in range(2):
-        turned = jnp.concatenate([p_three[which, 0:448].T, p_three[which, 448:896].T], 0)
-        partial = folded(jnp.dot(turned, factor, preferred_element_type=F32))
+        partial = inner_terms(which, 768, 64, l_three[384:448])
         for piece in range(8):
-            sums[8 * which + piece] = partial[32 * piece:32 * piece + 32]
+            sums[8 * which + piece] = sums[8 * which + piece] + partial[32 * piece:32 * piece + 32]
     final = []
     for hop in range(1, 16):
         target = wrap(r + hop, 16)
@@ -470,10 +565,13 @@
         total = total + gained[source]
     out_three[0, 448:480] = d_three[...].astype(F32) - total
 
-    swap.wait_send()
-    for group in [one, two, three, ring, s01, s11, s02, s12, s22, t01, t02, t12]:
+    first_swap.wait_send()
+    last_swap.wait_send()
+    for group in [one, two, three, ring, *s01, s11, s02, s12, s22, *t01, t02, t12]:
         for copy in group.started:
             copy.wait_send()
+    for group in [*s01, s11]:
+        group.drain()
     for copy in final:
         copy.wait_send()
 
@@ -498,17 +596,18 @@
             pltpu.VMEM((4, 4, 256, 256), BF16),
             pltpu.VMEM((4, 4, 384, 256), BF16),
             pltpu.VMEM((4, 4, 448, 256), BF16),
-            pltpu.VMEM((16, 128, 256), BF16),
+            pltpu.VMEM((2, 16, 128, 128), BF16),
             pltpu.VMEM((16, 64, 256), BF16),
             pltpu.VMEM((16, 64, 128), BF16),
             pltpu.VMEM((16, 32, 256), F32),
             pltpu.VMEM((16, 32, 256), F32),
             dma((3, 4, 4)), dma((3, 4, 4)),
             dma((4, 2)), dma((4, 2)), dma((8,)), dma((8,)),
-            dma((5, 4)), dma((5, 4)), dma((5, 4)), dma((5, 4)),
-            dma((3, 16)), dma((3, 16)), dma((3,)), dma((3,)),
+            dma((3, 2)), dma((3, 2)), dma((3, 2)), dma((3, 2)),
+            dma((3, 5)), dma((3, 3)), dma((3, 4)), dma((3, 4)), dma((2,)), dma((2,)),
+            dma((4, 16)), dma((4, 16)), dma((4,)), dma((4,)),
             dma((16,)), dma((16,)),
-            dma((7,)),
+            dma((8,)),
         ],
         compiler_params=pltpu.CompilerParams(
             collective_id=0, has_side_effects=True, vmem_limit_bytes=60 * 1024 * 1024

time: 137 us -> 129 us (0.942)
  Pallas kernels: 130 us -> 123 us
    pallas_call x1, Pallas kernels: 130 us -> 123 us  [per_device(): pl.pallas_call(kernel, out_shape=(jax.ShapeDtypeStruct((1, 384, 256), F32...]
where the time goes in v2:
time: 129 us; the launch traced here: 128 us
  Pallas kernels  123 us (95%)
  local copies, waits for them, and re-layouts  3.8 us (3%)
    pallas_call x1, Pallas kernels, per_device(): pl.pallas_call(kernel, out_shape=(jax.ShapeDtypeStruct((1, 384, 256), F32...  123 us
    unnamed x7, local copies, waits for them, and re-layouts  3.8 us

profile of v2, /device:TPU:24, one launch (start us, length us, event | category | flops | bytes accessed | tf_op | source)
XLA Modules:
  0.0 127.7 jit_solution(5306267181620890523)
XLA Ops:
  0.6 123.2 %shard_map.94 = (f32[1,384,256]{2,1,0:T(8,128)}, f32[1,448,256]{2,1,0:T(8,128)}, f32[1,480,256]{2,1,0:T(8,128)}) custom-call(bf16[256,256]{1,0:T(8,128)(2,1)} %bitcast.9, bf16[256,256]{1,0:T(8,128)(2,1)} %bitcast.10, bf16[384,256]{1,0:T(8,128)(2,1)} %bitcast.8, bf16[448,256]{1,0:T(8,128)(2,1)} %bitcast.7, bf16[128,256]{1,0:T(8,128)(2,1)} %bitcast.11, ...), custom_call_target="tpu_custom_call" | custom-call | tf_op jit(solution)/shard_map/pallas_call | solution.py:582
  123.9 0.0 copy-start.1
  123.9 1.8 %copy.13 = f32[1,384,256]{2,1,0:T(8,128)} copy(f32[1,384,256]{2,1,0:T(8,128)} %get-tuple-element.6) | data formatting | bytes 786432
  125.7 0.0 copy-done.1
  125.7 0.0 copy-start
  125.7 0.8 copy.14
  126.5 0.4 copy-done
  126.9 0.8 copy.15
Async XLA Ops:
  123.9 1.8 %copy-start.1 = (f32[1,448,256]{2,1,0:T(8,128)S(1)}, f32[1,448,256]{2,1,0:T(8,128)}, u32[]{:S(2)}) copy-start(f32[1,448,256]{2,1,0:T(8,128)} %get-tuple-element.7) | copy-start | bytes 1376260
  125.7 1.2 copy-start

commit v3 on v2

--- a/solution.py
+++ b/solution.py
@@ -315,8 +315,8 @@
 
 
 class Turn:
-    def __init__(self, source, place, whole, send, recv, partner_send, partner_recv, local, at):
-        self.source, self.place, self.whole = source, place, whole
+    def __init__(self, source, place, send, recv, partner_send, partner_recv, local, at):
+        self.source, self.place = source, place
         self.send, self.recv, self.partner_send, self.partner_recv, self.local = send, recv, partner_send, partner_recv, local
         self.r, self.c, self.core = at
         self.started = []
@@ -330,31 +330,47 @@
             copy.start()
             self.started.append(copy)
 
+    def share(self, hop):
+        part = self.place(wrap(self.r - hop, 16), self.core)
+        copy = remote(part, part, self.partner_send.at[hop], self.partner_recv.at[hop], (self.r, self.c + 1 - 2 * self.core))
+        copy.start()
+        self.started.append(copy)
+
     def relay(self):
+        self.own.wait()
+        self.share(0)
         for hop in range(1, 16):
             part = self.place(wrap(self.r - hop, 16), self.core)
             remote(part, part, self.send.at[hop], self.recv.at[hop], (wrap(self.r + 1, 16), self.c)).wait_recv()
-        self.own.wait()
-        part = self.whole(self.core)
-        copy = remote(part, part, self.partner_send, self.partner_recv, (self.r, self.c + 1 - 2 * self.core))
-        copy.start()
-        self.started.append(copy)
+            self.share(hop)
 
     def finish(self):
-        part = self.whole(1 - self.core)
-        remote(part, part, self.partner_send, self.partner_recv, (self.r, self.c + 1 - 2 * self.core)).wait_recv()
-
-
-def kernel(root, l_one, l_two, l_three, d_one, d_two, d_three, out_one, out_two, out_three,
-           p_zero, p_one, p_two, p_three, g_one, g_two, g_three, turn_one, turn_two, turn_cross, sums, gained,
+        for hop in range(16):
+            part = self.place(wrap(self.r - hop, 16), 1 - self.core)
+            remote(part, part, self.partner_send.at[hop], self.partner_recv.at[hop],
+                   (self.r, self.c + 1 - 2 * self.core)).wait_recv()
+
+
+def kernel(root_in, l_one_in, l_two_in, l_three_in, d_one_in, d_two_in, d_three_in, out_one, out_two, out_three,
+           root, l_one, l_two, l_three, d_one, d_two, d_three, p_zero, p_one, p_two, p_three, g_one, g_two, g_three, turn_one, turn_two, turn_cross, sums, gained,
            plane_send, plane_recv, ring_send, ring_recv, ring_core_send, ring_core_recv,
            node_send, node_recv, node_core_send, node_core_recv,
            chain_send, chain_recv, chain_core_send, chain_core_recv, swap_send, swap_recv,
-           turn_send, turn_recv, turn_core_send, turn_core_recv, last_send, last_recv, local):
+           turn_send, turn_recv, turn_core_send, turn_core_recv, last_send, last_recv, local, fetched):
     r, c = lax.axis_index("row"), lax.axis_index("col")
     x, y = lax.div(r, 4), lax.rem(r, 4)
     z, core = lax.div(c, 2), lax.rem(c, 2)
     eighth, quarter = lax.rem(c, 8), lax.rem(c, 4)
+
+    fetches = [
+        pltpu.make_async_copy(source, held, fetched.at[index])
+        for index, (source, held) in enumerate([
+            (l_one_in, l_one), (root_in, root), (l_two_in, l_two), (l_three_in, l_three),
+            (d_one_in, d_one), (d_two_in, d_two), (d_three_in, d_three),
+        ])
+    ]
+    for fetch in fetches:
+        fetch.start()
 
     barrier = pltpu.get_barrier_semaphore()
     for hop in range(1, 16):
@@ -363,6 +379,8 @@
         pl.semaphore_signal(barrier, inc=1, device_id=(r, wrap(z + hop, 8) * 2 + core), device_id_type=MESH)
     pl.semaphore_signal(barrier, inc=1, device_id=(r, z * 2 + 1 - core), device_id_type=MESH)
     pl.semaphore_wait(barrier, 23)
+    for fetch in fetches:
+        fetch.wait()
 
     planes = [
         Plane(source, held, plane_send.at[level], plane_recv.at[level], local.at[level], (x, y, c))
@@ -385,8 +403,8 @@
     s12 = node(1, p_two, slice(512, 768), 2)
     s22 = node(2, p_two, slice(768, 896), 2)
 
-    def turn(index, source, place, whole):
-        return Turn(source, place, whole, turn_send.at[index], turn_recv.at[index], turn_core_send.at[index],
+    def turn(index, source, place):
+        return Turn(source, place, turn_send.at[index], turn_recv.at[index], turn_core_send.at[index],
                     turn_core_recv.at[index], local.at[4 + index], (r, c, core))
 
     def rows_at(start, size, which):
@@ -394,16 +412,13 @@
 
     def half_turn(half):
         lanes = slice(128 * half, 128 * half + 128)
-        return turn(2 + half, turn_one.at[half], lambda run, which: p_zero.at[run, rows_at(256, 128, which), lanes],
-                    lambda which: p_zero.at[:, rows_at(256, 128, which), lanes])
+        return turn(2 + half, turn_one.at[half], lambda run, which: p_zero.at[run, rows_at(256, 128, which), lanes])
 
     t01 = [half_turn(0), half_turn(1)]
-    t02 = turn(0, turn_two, lambda run, which: p_zero.at[run, rows_at(512, 64, which)],
-               lambda which: p_zero.at[:, rows_at(512, 64, which)])
+    t02 = turn(0, turn_two, lambda run, which: p_zero.at[run, rows_at(512, 64, which)])
     t12 = turn(1, turn_cross,
                lambda run, which: p_one.at[lax.div(run, 2), rows_at(768, 64, which),
-                                           pl.ds(pl.multiple_of(lax.rem(run, 2) * 128, 128), 128)],
-               lambda which: p_one.at[:, rows_at(768, 64, which)])
+                                           pl.ds(pl.multiple_of(lax.rem(run, 2) * 128, 128), 128)])
 
     def store(held, index, start, value):
         rows = value.shape[0]
@@ -582,13 +597,20 @@
     return pl.pallas_call(
         kernel,
         out_shape=(
-            jax.ShapeDtypeStruct((1, 384, 256), F32),
-            jax.ShapeDtypeStruct((1, 448, 256), F32),
-            jax.ShapeDtypeStruct((1, 480, 256), F32),
+            pltpu.VMEM((1, 384, 256), F32),
+            pltpu.VMEM((1, 448, 256), F32),
+            pltpu.VMEM((1, 480, 256), F32),
         ),
-        in_specs=[vmem] * 7,
+        in_specs=[pl.BlockSpec(memory_space=pl.ANY)] * 7,
         out_specs=(vmem, vmem, vmem),
         scratch_shapes=[
+            pltpu.VMEM((256, 256), BF16),
+            pltpu.VMEM((256, 256), BF16),
+            pltpu.VMEM((384, 256), BF16),
+            pltpu.VMEM((448, 256), BF16),
+            pltpu.VMEM((128, 256), BF16),
+            pltpu.VMEM((64, 256), BF16),
+            pltpu.VMEM((32, 256), BF16),
             pltpu.VMEM((16, 640, 256), BF16),
             pltpu.VMEM((8, 896, 256), BF16),
             pltpu.VMEM((4, 896, 256), BF16),
@@ -605,9 +627,9 @@
             dma((4, 2)), dma((4, 2)), dma((8,)), dma((8,)),
             dma((3, 2)), dma((3, 2)), dma((3, 2)), dma((3, 2)),
             dma((3, 5)), dma((3, 3)), dma((3, 4)), dma((3, 4)), dma((2,)), dma((2,)),
-            dma((4, 16)), dma((4, 16)), dma((4,)), dma((4,)),
+            dma((4, 16)), dma((4, 16)), dma((4, 16)), dma((4, 16)),
             dma((16,)), dma((16,)),
-            dma((8,)),
+            dma((8,)), dma((7,)),
         ],
         compiler_params=pltpu.CompilerParams(
             collective_id=0, has_side_effects=True, vmem_limit_bytes=60 * 1024 * 1024

time: 129 us -> 126 us (0.977)
  local copies, waits for them, and re-layouts: 3.8 us -> 2.29 us
    unnamed x7 -> x3, local copies, waits for them, and re-layouts: 3.8 us -> 2.29 us
where the time goes in v3:
time: 126 us
  Pallas kernels  123 us (98%)
  local copies, waits for them, and re-layouts  2.29 us (2%)
    pallas_call x1, Pallas kernels, per_device(): pl.pallas_call(kernel, out_shape=(pltpu.VMEM((1, 384, 256), F32), pltpu.V...  123 us

profile of v3, /device:TPU:24, one launch (start us, length us, event | category | flops | bytes accessed | tf_op | source)
XLA Modules:
  0.0 125.6 jit_solution(17649118374642590585)
XLA Ops:
  0.6 122.7 %shard_map.94 = (f32[1,384,256]{2,1,0:T(8,128)S(1)}, f32[1,448,256]{2,1,0:T(8,128)S(1)}, f32[1,480,256]{2,1,0:T(8,128)S(1)}) custom-call(bf16[256,256]{1,0:T(8,128)(2,1)} %bitcast.9, bf16[256,256]{1,0:T(8,128)(2,1)} %bitcast.10, bf16[384,256]{1,0:T(8,128)(2,1)} %bitcast.8, bf16[448,256]{1,0:T(8,128)(2,1)} %bitcast.7, bf16[128,256]{1,0:T(8,128)(2,1)} %bitcast.11, ...), custom_call_target="tpu_custom_call" | custom-call | tf_op jit(solution)/shard_map/pallas_call | solution.py:597
  123.3 0.7 copy.13
  124.1 0.8 copy.14
  124.9 0.8 copy.15

commit v4 on v3

--- a/solution.py
+++ b/solution.py
@@ -497,13 +497,21 @@
             turn_two[4 * k + piece] = turned[64 * piece:64 * piece + 64]
     t02.open()
 
+    early = zero_part(two, 256, 512)
     s11.relay()
     s11.finish()
-    value = -folded(zero_part(two, 256, 512) + one_part(two, 512, 768))
+    value = -folded(early + one_part(two, 512, 768))
     store(p_two, quarter, 512, value)
     s12.open()
     out_two[0, 256:384] = value
 
+    three.finish()
+    upper = -(zero_part(three, 0, 256) + folded_halves(one_part(three, 0, 512)) + folded(two_part(three, 0, 512)))
+    out_three[0, 0:256] = upper
+    high, low = halves(upper)
+    p_three[core, 0:256] = high
+    p_three[core, 384:640] = low
+    early = zero_part(three, 256, 512) + one_part(three, 512, 768)
     s12.relay()
     s12.finish()
     for k in range(4):
@@ -513,13 +521,7 @@
             turn_cross[4 * k + piece] = turned[64 * piece:64 * piece + 64]
     t12.open()
 
-    three.finish()
-    upper = -(zero_part(three, 0, 256) + folded_halves(one_part(three, 0, 512)) + folded(two_part(three, 0, 512)))
-    out_three[0, 0:256] = upper
-    high, low = halves(upper)
-    p_three[core, 0:256] = high
-    p_three[core, 384:640] = low
-    middle = -folded(zero_part(three, 256, 512) + one_part(three, 512, 768) + two_part(three, 512, 768))
+    middle = -folded(early + two_part(three, 512, 768))
     out_three[0, 256:384] = middle
     high, low = halves(middle)
     p_three[core, 256:384] = high
@@ -541,8 +543,9 @@
     t02.relay()
     t12.relay()
     t02.finish()
+    early = zero_part(two, 512, 640)
     t12.finish()
-    value = d_two[...].astype(F32) - folded(zero_part(two, 512, 640) + one_part(two, 768, 896))
+    value = d_two[...].astype(F32) - folded(early + one_part(two, 768, 896))
     store(p_two, quarter, 768, value)
     s22.open()
     out_two[0, 384:448] = value
@@ -551,10 +554,11 @@
         partial = inner_terms(which, 0, 384, l_three[0:384])
         for piece in range(8):
             sums[8 * which + piece] = partial[32 * piece:32 * piece + 32]
+    early = zero_part(three, 512, 640) + one_part(three, 768, 896)
     s22.relay()
     s22.finish()
 
-    lower = -folded(zero_part(three, 512, 640) + one_part(three, 768, 896) + two_part(three, 768, 896))
+    lower = -folded(early + two_part(three, 768, 896))
     high, low = halves(lower)
     p_three[core, 768:832] = high
     p_three[core, 832:896] = low

time: 126 us -> 125 us (level)
  no operation moved by 1% of the time
where the time goes in v4:
time: 125 us
  Pallas kernels  122 us (98%)
  local copies, waits for them, and re-layouts  2.29 us (2%)
    pallas_call x1, Pallas kernels, per_device(): pl.pallas_call(kernel, out_shape=(pltpu.VMEM((1, 384, 256), F32), pltpu.V...  122 us

profile of v4, /device:TPU:24, one launch (start us, length us, event | category | flops | bytes accessed | tf_op | source)
XLA Modules:
  0.0 125.0 jit_solution(129551779882777294)
XLA Ops:
  0.6 122.0 %shard_map.94 = (f32[1,384,256]{2,1,0:T(8,128)S(1)}, f32[1,448,256]{2,1,0:T(8,128)S(1)}, f32[1,480,256]{2,1,0:T(8,128)S(1)}) custom-call(bf16[256,256]{1,0:T(8,128)(2,1)} %bitcast.9, bf16[256,256]{1,0:T(8,128)(2,1)} %bitcast.10, bf16[384,256]{1,0:T(8,128)(2,1)} %bitcast.8, bf16[448,256]{1,0:T(8,128)(2,1)} %bitcast.7, bf16[128,256]{1,0:T(8,128)(2,1)} %bitcast.11, ...), custom_call_target="tpu_custom_call" | custom-call | tf_op jit(solution)/shard_map/pallas_call | solution.py:601
  122.7 0.7 copy.13
  123.4 0.8 copy.14
  124.2 0.8 copy.15

commit v5 on v4

--- a/solution.py
+++ b/solution.py
@@ -477,6 +477,7 @@
     store(p_two, quarter, 0, value)
     s02.open()
     out_two[0, 0:256] = value
+    three.close()
 
     for half in range(2):
         t01[half].relay()
@@ -487,7 +488,6 @@
     s11.open()
     out_one[0, 256:384] = value
 
-    three.close()
     s02.relay()
     s02.finish()
     for k in range(4):

time: 125 us -> 125 us (level)
  no operation moved by 1% of the time
where the time goes in v5:
time: 125 us
  Pallas kernels  122 us (98%)
  local copies, waits for them, and re-layouts  2.29 us (2%)
    pallas_call x1, Pallas kernels, per_device(): pl.pallas_call(kernel, out_shape=(pltpu.VMEM((1, 384, 256), F32), pltpu.V...  122 us

profile of v5, /device:TPU:24, one launch (start us, length us, event | category | flops | bytes accessed | tf_op | source)
XLA Modules:
  0.0 124.9 jit_solution(12783899928099055649)
XLA Ops:
  0.6 122.0 %shard_map.94 = (f32[1,384,256]{2,1,0:T(8,128)S(1)}, f32[1,448,256]{2,1,0:T(8,128)S(1)}, f32[1,480,256]{2,1,0:T(8,128)S(1)}) custom-call(bf16[256,256]{1,0:T(8,128)(2,1)} %bitcast.9, bf16[256,256]{1,0:T(8,128)(2,1)} %bitcast.10, bf16[384,256]{1,0:T(8,128)(2,1)} %bitcast.8, bf16[448,256]{1,0:T(8,128)(2,1)} %bitcast.7, bf16[128,256]{1,0:T(8,128)(2,1)} %bitcast.11, ...), custom_call_target="tpu_custom_call" | custom-call | tf_op jit(solution)/shard_map/pallas_call | solution.py:601
  122.6 0.7 copy.13
  123.3 0.8 copy.14
  124.1 0.8 copy.15
